TPU v7x, 32 devices: a whole 2x2x4 slice. The times are simulated.
32 devices in a mesh: cyc: 4 (over z), tile: 8 (over y, x, core).
Axes of the slice: x: 2, y: 2, z: 4, core: 2. Of those that a mesh axis runs over, the one named last changes fastest.
Arguments:
- weight_change: bfloat16 [4, 80, 80, 256], P('cyc', None, None, 'tile'), may hold values from -0.1796875 to 0.1796875
- ensemble: bfloat16 [4, 80, 8, 4096], P('cyc', None, None, 'tile'), may hold values from -6 to 6
- stencil_index: int32 [4, 4096], P(None, 'tile'), may hold values from 0 to 39
- stencil_weight: float32 [4, 4096], P(None, 'tile'), may hold values from 0.1 to 1
Outputs:
- smoothed: bfloat16 [4, 80, 8, 4096], P('cyc', None, None, 'tile')
Inputs may be any that keep to these rules, and one draw needn't show every extreme that they name: `stencil_index`: positions 0 to 3 of the extended list are the last columns of the sector before (periodic in longitude), positions 36 and beyond the first columns of the sector after.
All inputs are finite; a program needn't handle non-finite values.
Results may differ from a plain program's by a relative error of at most 0.0085.
Values may be sent and summed in bfloat16 or wider, within the bound.
A program may use at most 128 MiB of HBM per device.

v0:
```python
import math

import jax
import jax.numpy as jnp
from jax import lax
from jax.sharding import PartitionSpec as P

RIM_COLS = 4


def with_halo(block, sides, width):
    for axis, dim in sides:
        count = lax.axis_size(axis)
        forward = [(i, i + 1) for i in range(count - 1)]
        forward.append((count - 1, 0))
        backward = [(target, source) for source, target in forward]
        low = lax.ppermute(
            lax.slice_in_dim(block, block.shape[dim] - width, None, axis=dim), axis, forward
        )
        high = lax.ppermute(lax.slice_in_dim(block, 0, width, axis=dim), axis, backward)
        block = jnp.concatenate([low, block, high], axis=dim)
    return block


def combine(earlier, later):
    return jnp.einsum(
        "ijg,jkg->ikg",
        later,
        earlier,
        precision=lax.Precision.HIGHEST,
        preferred_element_type=jnp.float32,
    )


def suffix_of(raw, eye):
    mats = raw.astype(jnp.float32) + eye
    unity = jnp.broadcast_to(eye, mats.shape)
    every = lax.all_gather(raw[None], "cyc", axis=0, tiled=True)
    count = every.shape[0]
    mine = lax.axis_index("cyc")

    def step(number, carry):
        later_cycle = count - 1 - number
        weight = (
            lax.dynamic_index_in_dim(every, later_cycle, 0, keepdims=False).astype(jnp.float32)
            + eye
        )
        product = combine(carry, weight)
        return jnp.where(later_cycle > mine, product, carry)

    return lax.fori_loop(0, count, step, unity)


def on_device(weight_change, ensemble, stencil_index, stencil_weight):
    members = weight_change.shape[1]
    eye = jnp.eye(members, dtype=jnp.float32)[:, :, None]
    suffix = suffix_of(weight_change[0], eye)
    extended = with_halo(suffix, (("tile", 2),), RIM_COLS)
    width = extended.shape[2]
    flat = extended.reshape(members * members, width)
    shares = stencil_weight / jnp.sum(stencil_weight, axis=0, keepdims=True)
    states = ensemble[0]
    points = states.shape[2]
    block = math.gcd(points, 256)
    blocks = points // block
    slots = jnp.arange(width)[:, None]

    def one_block(number, output):
        begin = number * block
        index = lax.dynamic_slice_in_dim(stencil_index, begin, block, 1)
        weights = lax.dynamic_slice_in_dim(shares, begin, block, 1)
        table = jnp.zeros((width, block), jnp.float32)
        for corner in range(4):
            table = table + jnp.where(
                index[corner][None, :] == slots, weights[corner][None, :], 0.0
            )
        interp = jnp.dot(
            flat, table, precision=lax.Precision.HIGHEST, preferred_element_type=jnp.float32
        )
        interp = interp.reshape(members, members, block).astype(jnp.bfloat16)
        piece = lax.dynamic_slice_in_dim(states, begin, block, 2)
        mixed = jnp.einsum(
            "nvf,nmf->mvf", piece, interp, preferred_element_type=jnp.float32
        ).astype(jnp.bfloat16)
        return lax.dynamic_update_slice_in_dim(output, mixed, begin, 2)

    result = lax.fori_loop(0, blocks, one_block, jnp.zeros_like(states))
    return result[None]


def solution(mesh):
    placed = (
        P("cyc", None, None, "tile"),
        P("cyc", None, None, "tile"),
        P(None, "tile"),
        P(None, "tile"),
    )
    return jax.shard_map(
        on_device,
        mesh=mesh,
        in_specs=placed,
        out_specs=P("cyc", None, None, "tile"),
        check_vma=False,
    )
```

profile of v0, /device:TPU:0, one launch (start us, length us, event | category | flops | bytes accessed | tf_op | source)
XLA Modules:
  0.0 144.7 jit_solution(10751139140478643147)
XLA Ops:
  6.5 0.7 all-gather.2.cloned.1.call-update
  7.3 0.7 reduce_sum.9
  8.0 58.4 %all-gather.2.cloned.1.call-done = bf16[4,80,80,32]{2,3,1,0:T(8,128)(2,1)} async-done(((bf16[1,80,80,32]{2,3,1,0:T(8,128)(2,1)}), bf16[4,80,80,32]{2,3,1,0:T(8,128)(2,1)}) %all-gather.2.cloned.1.call-update) | async-done | bytes 1638416 | tf_op jit(solution)/shard_map/all_gather | solution.py:38
  66.5 11.8 %while.31 = (s32[]{:T(128)}, f32[80,80,32]{1,0,2:T(8,128)S(1)}, s32[]{:T(128)}, bf16[4,80,80,32]{2,3,1,0:T(8,128)(2,1)}, s32[]{:T(128)}, /*index=5*/s32[]{:T(128)}, s32[]{:T(128)}, s32[]{:T(128)}) while((s32[]{:T(128)}, f32[80,80,32]{1,0,2:T(8,128)S(1)}, s32[]{:T(128)}, bf16[4,80,80,32]{2,3,1,0:T(8,128)(2,1)}, s32[]{:T(128)}, ...), condition=%wide.region_2.3_spmd.clone, body=%wide.region_1.2_spmd.clone.sunk | while | flops 197235200 | bytes 4556953 | solution.py:51
  66.5 0.1 copy.50
  66.6 1.2 constant_dynamic-slice_fusion.6
  67.8 1.7 %fusion.41 = f32[80,80,32]{1,0,2:T(8,128)S(1)} fusion(f32[80,80,32]{1,0,2:T(8,128)S(1)} %copy.50, bf16[1,80,80,32]{2,3,1,0:T(8,128)(2,1)S(1)} %constant_dynamic-slice_fusion.6, f32[80,80]{1,0:T(8,128)S(1)} %convert_bitcast_fusion.2, pred[]{:T(512)S(6)} %gt.12), kind=kOutput, calls=%fused_computation.3.clone.1 | convolution fusion | flops 197222400 | bytes 2073601 | tf_op jit(solution)/shard_map/while/body/eval_jaxpr/ijg,jkg->ikg/dot_general | solution.py:26
  69.6 1.1 constant_dynamic-slice_fusion.6
  70.8 1.7 %fusion.41 = f32[80,80,32]{1,0,2:T(8,128)S(1)} fusion(f32[80,80,32]{1,0,2:T(8,128)S(1)} %copy.50, bf16[1,80,80,32]{2,3,1,0:T(8,128)(2,1)S(1)} %constant_dynamic-slice_fusion.6, f32[80,80]{1,0:T(8,128)S(1)} %convert_bitcast_fusion.2, pred[]{:T(512)S(6)} %gt.12), kind=kOutput, calls=%fused_computation.3.clone.1 | convolution fusion | flops 197222400 | bytes 2073601 | tf_op jit(solution)/shard_map/while/body/eval_jaxpr/ijg,jkg->ikg/dot_general | solution.py:26
  72.6 1.1 constant_dynamic-slice_fusion.6
  73.7 1.7 %fusion.41 = f32[80,80,32]{1,0,2:T(8,128)S(1)} fusion(f32[80,80,32]{1,0,2:T(8,128)S(1)} %copy.50, bf16[1,80,80,32]{2,3,1,0:T(8,128)(2,1)S(1)} %constant_dynamic-slice_fusion.6, f32[80,80]{1,0:T(8,128)S(1)} %convert_bitcast_fusion.2, pred[]{:T(512)S(6)} %gt.12), kind=kOutput, calls=%fused_computation.3.clone.1 | convolution fusion | flops 197222400 | bytes 2073601 | tf_op jit(solution)/shard_map/while/body/eval_jaxpr/ijg,jkg->ikg/dot_general | solution.py:26
  75.5 1.1 constant_dynamic-slice_fusion.6
  76.7 1.7 %fusion.41 = f32[80,80,32]{1,0,2:T(8,128)S(1)} fusion(f32[80,80,32]{1,0,2:T(8,128)S(1)} %copy.50, bf16[1,80,80,32]{2,3,1,0:T(8,128)(2,1)S(1)} %constant_dynamic-slice_fusion.6, f32[80,80]{1,0:T(8,128)S(1)} %convert_bitcast_fusion.2, pred[]{:T(512)S(6)} %gt.12), kind=kOutput, calls=%fused_computation.3.clone.1 | convolution fusion | flops 197222400 | bytes 2073601 | tf_op jit(solution)/shard_map/while/body/eval_jaxpr/ijg,jkg->ikg/dot_general | solution.py:26
  78.5 2.6 %collective-permute-start.1 = (f32[80,80,4]{1,0,2:T(8,128)S(1)}, f32[80,80,4]{1,0,2:T(8,128)S(1)}, u32[]{:S(2)}, u32[]{:S(2)}) collective-permute-start(f32[80,80,4]{1,0,2:T(8,128)S(1)} %get-tuple-element.349), channel_id=1, source_target_pairs={{1,0},{2,1},{3,2},{4,3},{5,4},{6,5},{7,6},{0,7},{9,8},{10,9},{11,1... | collective-permute-start | bytes 307208 | tf_op jit(solution)/shard_map/ppermute | solution.py:20
  81.1 1.7 %copy.19 = bf16[1,80,8,512]{1,2,3,0:T(8,128)(2,1)} copy(bf16[1,80,8,512]{3,2,1,0:T(8,128)(2,1)S(1)} %copy-done.1) | data formatting | bytes 1310720 | tf_op args[1]
  82.9 1.2 collective-permute-done
  84.1 0.1 pad_maximum_fusion
  84.2 2.4 %copy.18 = f32[80,80,40]{2,1,0:T(8,128)} copy(f32[80,80,40]{1,0,2:T(8,128)S(1)} %pad_maximum_fusion) | data formatting | bytes 2048000 | tf_op jit(solution)/shard_map/concatenate | solution.py:21
  86.6 0.9 broadcast_in_dim.96.clone
  87.5 50.4 %while.32 = (s32[]{:T(128)}, bf16[80,8,512]{2,1,0:T(8,128)(2,1)}, s32[4,512]{1,0:T(4,128)S(1)}, f32[4,512]{1,0:T(4,128)S(1)}, f32[6400,40]{1,0:T(8,128)}, /*inde...) while((s32[]{:T(128)}, bf16[80,8,512]{2,1,0:T(8,128)(2,1)}, ...), condition=%wide.region_4.5_spmd.clone.clone, body=%wide.region_3.4_spmd.clone.clone.sunk | while | flops 814561280 | bytes 30736716 | solution.py:87
  87.6 8.2 %fusion.46 = bf16[6400,256]{0,1:T(8,128)(2,1)S(1)} fusion(f32[6400,40]{1,0:T(8,128)} %get-tuple-element.482, f32[256]{0:T(256)S(1)} %bitcast.71, s32[256]{0:T(256)S(1)} %bitcast.75, f32[256]{0:T(256)S(1)} %bitcast.69, s32[256]{0:T(256)S(1)} %bitcast.73, f32[256]{0:T(256)S(1)} %bitcast.70, s32[256]{0:T(256)S(1)} %bitcast.74, f32[256]{0:T(256)S(1)} %bitcast.68, ...), kind=kOutput, calls=%fused_computation.11.clone.1 | convolution fusion | flops 788183040 | bytes 4308992 | tf_op jit(solution)/shard_map/while/body/eval_jaxpr/dot_general | solution.py:77
  95.8 3.5 %copy.33 = bf16[6400,256]{1,0:T(8,128)(2,1)} copy(bf16[6400,256]{0,1:T(8,128)(2,1)S(1)} %fusion.46) | data formatting | bytes 6553600 | tf_op jit(solution)/shard_map/while/body/eval_jaxpr/convert_element_type | solution.py:80
  99.3 8.0 %copy.34 = bf16[80,80,256]{1,0,2:T(8,128)(2,1)} copy(bf16[80,80,256]{2,1,0:T(8,128)(2,1)} %bitcast.65) | data formatting | bytes 6553600 | tf_op jit(solution)/shard_map/while/body/eval_jaxpr/convert_element_type | solution.py:80
  107.3 4.0 %fusion.47 = bf16[80,8,256]{0,1,2:T(8,128)(2,1)S(1)} fusion(bf16[80,80,256]{1,0,2:T(8,128)(2,1)} %copy.34, bf16[80,8,512]{0,1,2:T(8,128)(2,1)S(1)} %copy-done, s32[]{:T(128)S(6)} %select_n.118), kind=kOutput, calls=%fused_computation.13.clone.1 | convolution fusion | flops 26378240 | bytes 4128772 | tf_op jit(solution)/shard_map/while/body/eval_jaxpr/nvf,nmf->mvf/dot_general | solution.py:82
  111.3 0.5 copy.35
  111.9 0.8 copy-done.3
  112.9 8.2 %fusion.46 = bf16[6400,256]{0,1:T(8,128)(2,1)S(1)} fusion(f32[6400,40]{1,0:T(8,128)} %get-tuple-element.482, f32[256]{0:T(256)S(1)} %bitcast.71, s32[256]{0:T(256)S(1)} %bitcast.75, f32[256]{0:T(256)S(1)} %bitcast.69, s32[256]{0:T(256)S(1)} %bitcast.73, f32[256]{0:T(256)S(1)} %bitcast.70, s32[256]{0:T(256)S(1)} %bitcast.74, f32[256]{0:T(256)S(1)} %bitcast.68, ...), kind=kOutput, calls=%fused_computation.11.clone.1 | convolution fusion | flops 788183040 | bytes 4308992 | tf_op jit(solution)/shard_map/while/body/eval_jaxpr/dot_general | solution.py:77
  121.0 3.5 %copy.33 = bf16[6400,256]{1,0:T(8,128)(2,1)} copy(bf16[6400,256]{0,1:T(8,128)(2,1)S(1)} %fusion.46) | data formatting | bytes 6553600 | tf_op jit(solution)/shard_map/while/body/eval_jaxpr/convert_element_type | solution.py:80
  124.5 8.0 %copy.34 = bf16[80,80,256]{1,0,2:T(8,128)(2,1)} copy(bf16[80,80,256]{2,1,0:T(8,128)(2,1)} %bitcast.65) | data formatting | bytes 6553600 | tf_op jit(solution)/shard_map/while/body/eval_jaxpr/convert_element_type | solution.py:80
  132.5 4.0 %fusion.47 = bf16[80,8,256]{0,1,2:T(8,128)(2,1)S(1)} fusion(bf16[80,80,256]{1,0,2:T(8,128)(2,1)} %copy.34, bf16[80,8,512]{0,1,2:T(8,128)(2,1)S(1)} %copy-done, s32[]{:T(128)S(6)} %select_n.118), kind=kOutput, calls=%fused_computation.13.clone.1 | convolution fusion | flops 26378240 | bytes 4128772 | tf_op jit(solution)/shard_map/while/body/eval_jaxpr/nvf,nmf->mvf/dot_general | solution.py:82
  136.5 0.5 copy.35
  137.1 0.8 copy-done.3
  (36 shorter events, 0.9 us)
Async XLA Ops:
  6.5 59.9 %all-gather.2.cloned.1.call-start = ((), (), s32[]{:S(2)}) async-start(), calls=%async_computation | async-start | bytes 3276800 | tf_op jit(solution)/shard_map/all_gather | solution.py:38
  66.5 14.6 %copy-start.5 = (f32[4,512]{1,0:T(4,128)S(1)}, f32[4,512]{1,0:T(4,128)}, u32[]{:S(2)}) copy-start(f32[4,512]{1,0:T(4,128)} %param.11) | copy-start | bytes 24580
  66.5 14.6 %copy-start.1 = (bf16[1,80,8,512]{3,2,1,0:T(8,128)(2,1)S(1)}, bf16[1,80,8,512]{3,2,1,0:T(8,128)(2,1)}, u32[]{:S(2)}) copy-start(bf16[1,80,8,512]{3,2,1,0:T(8,128)(2,1)} %param.9) | copy-start | bytes 1966084
  78.4 5.7 %collective-permute-start = (f32[80,80,4]{1,0,2:T(8,128)S(1)}, f32[80,80,4]{1,0,2:T(8,128)S(1)}, u32[]{:S(2)}, u32[]{:S(2)}) collective-permute-start(f32[80,80,4]{1,0,2:T(8,128)S(1)} %get-tuple-element.348), channel_id=1, source_target_pairs={{0,1},{1,2},{2,3},{3,4},{4,5},{5,6},{6,7},{7,0},{8,9},{9,10},{10,1... | collective-permute-start | bytes 307208 | tf_op jit(solution)/shard_map/ppermute | solution.py:17
  78.5 5.6 %collective-permute-start.1 = (f32[80,80,4]{1,0,2:T(8,128)S(1)}, f32[80,80,4]{1,0,2:T(8,128)S(1)}, u32[]{:S(2)}, u32[]{:S(2)}) collective-permute-start(f32[80,80,4]{1,0,2:T(8,128)S(1)} %get-tuple-element.349), channel_id=1, source_target_pairs={{1,0},{2,1},{3,2},{4,3},{5,4},{6,5},{7,6},{0,7},{9,8},{10,9},{11,1... | collective-permute-start | bytes 307208 | tf_op jit(solution)/shard_map/ppermute | solution.py:20
  84.2 3.3 %copy-start.4 = (s32[4,512]{1,0:T(4,128)S(1)}, s32[4,512]{1,0:T(4,128)}, u32[]{:S(2)}) copy-start(s32[4,512]{1,0:T(4,128)} %param.10) | copy-start | bytes 24580
  99.3 8.0 %copy-start = (bf16[80,8,512]{0,1,2:T(8,128)(2,1)S(1)}, bf16[80,8,512]{0,1,2:T(8,128)(2,1)}, u32[]{:S(2)}) copy-start(bf16[80,8,512]{0,1,2:T(8,128)(2,1)} %get-tuple-element.483) | copy-start | bytes 1966084 | tf_op jit(solution)/shard_map/while
  107.3 4.5 %copy-start.2 = (bf16[80,8,512]{2,1,0:T(8,128)(2,1)S(1)}, bf16[80,8,512]{2,1,0:T(8,128)(2,1)}, u32[]{:S(2)}) copy-start(bf16[80,8,512]{2,1,0:T(8,128)(2,1)} %get-tuple-element.466) | copy-start | bytes 1966084 | tf_op jit(solution)/shard_map/while
  111.9 0.8 copy-start.3
  124.5 8.0 %copy-start = (bf16[80,8,512]{0,1,2:T(8,128)(2,1)S(1)}, bf16[80,8,512]{0,1,2:T(8,128)(2,1)}, u32[]{:S(2)}) copy-start(bf16[80,8,512]{0,1,2:T(8,128)(2,1)} %get-tuple-element.483) | copy-start | bytes 1966084 | tf_op jit(solution)/shard_map/while
  132.5 4.5 %copy-start.2 = (bf16[80,8,512]{2,1,0:T(8,128)(2,1)S(1)}, bf16[80,8,512]{2,1,0:T(8,128)(2,1)}, u32[]{:S(2)}) copy-start(bf16[80,8,512]{2,1,0:T(8,128)(2,1)} %get-tuple-element.466) | copy-start | bytes 1966084 | tf_op jit(solution)/shard_map/while
  137.1 0.8 copy-start.3
Sparse Core Ops, SparseCore 0:
  8.9 57.4 all-gather.1
where the time goes:
time: 147 us; the launch traced here: 145 us
  waiting for transfers between devices  60.4 us (41%)
  local copies, waits for them, and re-layouts  36 us (24%)
  matrix products  31.1 us (21%)
  between operations  13.5 us (9%)
  starting transfers between devices  2.69 us (2%)
    all_gather x1, waiting for transfers between devices, suffix_of(): every = lax.all_gather(raw[None], 'cyc', axis=0, tiled=True)  58.4 us
    convert_element_type x4, local copies, waits for them, and re-layouts, one_block(): interp = interp.reshape(members, members, block).astype(jnp.bfloat16)  22.9 us
    dot_general x2, matrix products, one_block(): jnp.dot(flat, table, precision=lax.Precision.HIGHEST, preferred_element_t...  16.4 us
    dot_general x2, matrix products, one_block(): jnp.einsum('nvf,nmf->mvf', piece, interp, preferred_element_type=jnp.floa...  8.02 us
    dot_general x4, matrix products, combine(): jnp.einsum('ijg,jkg->ikg', later, earlier, precision=lax.Precision.HIGHES...  6.68 us
    dynamic_slice x4, local copies, waits for them, and re-layouts, step(): lax.dynamic_index_in_dim(every, later_cycle, 0, keepdims=False)  4.6 us
  transfers between devices with their start and end apart: 3, of which 2 were waited for; matrix products, arithmetic and copies ran while one was open for 2% of the time, Pallas kernels for 0%

commit v1 on v0

v1 whole, which is shorter than its diff:
```python
import functools

import jax
import jax.numpy as jnp
from jax import lax
from jax.experimental import pallas as pl
from jax.experimental.pallas import tpu as pltpu
from jax.sharding import PartitionSpec as P

RIM_COLS = 4
CHUNK = 8
MESH = pl.DeviceIdType.MESH


def round_up(value, step):
    return -(-value // step) * step


def plan_of(members, columns):
    half = round_up(RIM_COLS * members, 128)
    edge = [(i * members, i) for i in range(RIM_COLS)]
    edge += [(half + i * members, columns - RIM_COLS + i) for i in range(RIM_COLS)]
    chunks = [(0, 2 * half, edge)]
    start = 2 * half
    for first in range(RIM_COLS, columns - RIM_COLS, CHUNK):
        count = min(CHUNK, columns - RIM_COLS - first)
        width = round_up(count * members, 128)
        chunks.append((start, width, [(i * members, first + i) for i in range(count)]))
        start += width
    return half, chunks, start


def smoother(members, channels, columns, d_ref, ens_ref, idx_ref, wgt_ref, out_ref, *scratch):
    half, chunks, _ = plan_of(members, columns)
    held, sent, halo, table, total = scratch[:5]
    diag = scratch[5 : 5 + len(chunks)]
    send_sem, recv_sem, halo_send, halo_recv = scratch[5 + len(chunks) :]
    count, tiles = lax.axis_size("cyc"), lax.axis_size("tile")
    mine, tile = lax.axis_index("cyc"), lax.axis_index("tile")
    before, after = lax.rem(mine + count - 1, count), lax.rem(mine + 1, count)
    left, right = lax.rem(tile + tiles - 1, tiles), lax.rem(tile + 1, tiles)
    points = idx_ref.shape[1]

    barrier = pltpu.get_barrier_semaphore()
    for target in ({"cyc": before}, {"cyc": after}, {"tile": left}, {"tile": right}):
        pl.semaphore_signal(barrier, inc=1, device_id=target, device_id_type=MESH)
    pl.semaphore_wait(barrier, 4)

    def onward(number, source):
        start, width, _ = chunks[number]
        return pltpu.make_async_remote_copy(
            src_ref=source.at[:, pl.ds(start, width)],
            dst_ref=held.at[:, pl.ds(start, width)],
            send_sem=send_sem.at[number],
            recv_sem=recv_sem.at[number],
            device_id={"cyc": before},
            device_id_type=MESH,
        )

    def rim(side):
        return pltpu.make_async_remote_copy(
            src_ref=held.at[:, pl.ds(side * half, half)],
            dst_ref=halo.at[:, pl.ds((1 - side) * half, half)],
            send_sem=halo_send.at[side],
            recv_sem=halo_recv.at[side],
            device_id={"tile": (left, right)[side]},
            device_id_type=MESH,
        )

    last = mine == count - 1
    inner = jnp.logical_and(mine > 0, mine < count - 1)

    @pl.when(last)
    def _():
        for number in range(len(chunks)):
            onward(number, d_ref).start()

    @pl.when(inner)
    def _():
        for (start, width, parts), block in zip(chunks, diag):
            lane = lax.broadcasted_iota(jnp.int32, (members, width), 1)
            values = d_ref[:, start : start + width].astype(jnp.float32)
            block[...] = jnp.zeros_like(block)
            for offset, _ in parts:
                inside = jnp.logical_and(lane >= offset, lane < offset + members)
                block[offset : offset + members, :] = jnp.where(inside, values, 0.0).astype(
                    block.dtype
                )

    def apply(source, start, width, parts, first):
        ends = [offset for offset, _ in parts[1:]] + [width]

        def channel(number, carry):
            lanes = pl.ds(pl.multiple_of(number * points, points), points)
            states = ens_ref[:, lanes]
            rows = []
            for (offset, slot), end in zip(parts, ends):
                share = jnp.broadcast_to(table[slot : slot + 1, :], (members, points))
                rows.append(states * share.astype(states.dtype))
                if end > offset + members:
                    rows.append(jnp.zeros((end - offset - members, points), states.dtype))
            product = jnp.dot(
                source[:, start : start + width],
                jnp.concatenate(rows, axis=0),
                preferred_element_type=jnp.float32,
            )
            if first:
                total[:, lanes] = product + states.astype(jnp.float32)
            else:
                total[:, lanes] += product
            return carry

        lax.fori_loop(0, channels, channel, 0)

    @pl.when(jnp.logical_not(last))
    def _():
        weights = wgt_ref[...]
        shares = weights / jnp.sum(weights, axis=0, keepdims=True)
        slots = lax.broadcasted_iota(jnp.int32, table.shape, 0)
        entries = jnp.zeros(table.shape, jnp.float32)
        for corner in range(4):
            entries += jnp.where(
                idx_ref[corner : corner + 1, :] == slots, shares[corner : corner + 1, :], 0.0
            )
        table[...] = entries

    for number, (start, width, parts) in enumerate(chunks):

        @pl.when(jnp.logical_not(last))
        def _(number=number, start=start, width=width):
            onward(number, d_ref).wait_recv()
            if number == 0:
                rim(0).start()
                rim(1).start()

        @pl.when(inner)
        def _(number=number, start=start, width=width):
            lanes = slice(start, start + width)
            later = held[:, lanes]
            product = jnp.dot(later, diag[number][...], preferred_element_type=jnp.float32)
            product += later.astype(jnp.float32) + d_ref[:, lanes].astype(jnp.float32)
            sent[:, lanes] = product.astype(sent.dtype)
            onward(number, sent).start()

        @pl.when(jnp.logical_not(last))
        def _(number=number, start=start, width=width, parts=parts):
            apply(
                held, start, width, [(o, col + RIM_COLS) for o, col in parts], number == 0
            )

    @pl.when(jnp.logical_not(last))
    def _():
        rim(0).wait_recv()
        rim(1).wait_recv()
        parts = [(i * members, i) for i in range(RIM_COLS)]
        parts += [(half + i * members, RIM_COLS + columns + i) for i in range(RIM_COLS)]
        apply(halo, 0, 2 * half, parts, False)
        out_ref[...] = total[...].astype(out_ref.dtype)
        rim(0).wait_send()
        rim(1).wait_send()

    @pl.when(last)
    def _():
        out_ref[...] = ens_ref[...]

    @pl.when(mine > 0)
    def _():
        for number in range(len(chunks)):
            onward(number, d_ref).wait_send()


def on_device(weight_change, ensemble, stencil_index, stencil_weight):
    _, members, _, columns = weight_change.shape
    channels, points = ensemble.shape[2:]
    half, chunks, width = plan_of(members, columns)
    turned = jnp.transpose(weight_change[0], (1, 2, 0))
    pieces = []
    for begin, end in ((0, RIM_COLS), (columns - RIM_COLS, columns)):
        piece = turned[:, begin:end].reshape(members, RIM_COLS * members)
        pieces.append(jnp.pad(piece, ((0, 0), (0, half - piece.shape[1]))))
    for _, wide, parts in chunks[1:]:
        piece = turned[:, parts[0][1] : parts[-1][1] + 1].reshape(members, len(parts) * members)
        pieces.append(jnp.pad(piece, ((0, 0), (0, wide - piece.shape[1]))))
    packed = jnp.concatenate(pieces, axis=1)
    states = ensemble[0].reshape(members, channels * points)
    vmem = pl.BlockSpec(memory_space=pltpu.VMEM)
    result = pl.pallas_call(
        functools.partial(smoother, members, channels, columns),
        out_shape=jax.ShapeDtypeStruct(states.shape, states.dtype),
        in_specs=[vmem] * 4,
        out_specs=vmem,
        scratch_shapes=[
            pltpu.VMEM((members, width), jnp.bfloat16),
            pltpu.VMEM((members, width), jnp.bfloat16),
            pltpu.VMEM((members, 2 * half), jnp.bfloat16),
            pltpu.VMEM((columns + 2 * RIM_COLS, points), jnp.float32),
            pltpu.VMEM(states.shape, jnp.float32),
        ]
        + [pltpu.VMEM((wide, wide), jnp.bfloat16) for _, wide, _ in chunks]
        + [
            pltpu.SemaphoreType.DMA((len(chunks),)),
            pltpu.SemaphoreType.DMA((len(chunks),)),
            pltpu.SemaphoreType.DMA((2,)),
            pltpu.SemaphoreType.DMA((2,)),
        ],
        compiler_params=pltpu.CompilerParams(collective_id=0, has_side_effects=True),
    )(packed, states, stencil_index, stencil_weight)
    return result.reshape(1, members, channels, points)


def solution(mesh):
    placed = (
        P("cyc", None, None, "tile"),
        P("cyc", None, None, "tile"),
        P(None, "tile"),
        P(None, "tile"),
    )
    return jax.shard_map(
        on_device,
        mesh=mesh,
        in_specs=placed,
        out_specs=P("cyc", None, None, "tile"),
        check_vma=False,
    )
```

time: 147 us -> 39.7 us (0.27); the launches traced: 145 us -> 39.5 us
  waiting for transfers between devices: 60.4 us -> 0 us
  Pallas kernels: 0 us -> 32.6 us
  matrix products: 31.1 us -> 0 us
  local copies, waits for them, and re-layouts: 36 us -> 6.75 us
  between operations: 13.5 us -> 0.12 us
  starting transfers between devices: 2.69 us -> 0 us
    all_gather x1 -> x0, waiting for transfers between devices: 58.4 us -> none  [suffix_of(): every = lax.all_gather(raw[None], 'cyc', axis=0, tiled=True)]
    pallas_call x0 -> x1, Pallas kernels: none -> 32.6 us  [on_device(): pl.pallas_call(functools.partial(smoother, members, channels, columns), o...]
    dot_general x8 -> x0, matrix products: 31.1 us -> none  [the longest x2 16.4 us: one_block(): jnp.dot(flat, table, precision=lax.Precision.HIGHEST, preferred_element_t...]
    convert_element_type x4 -> x0, local copies, waits for them, and re-layouts: 22.9 us -> none  [one_block(): interp = interp.reshape(members, members, block).astype(jnp.bfloat16)]
    dynamic_slice x4 -> x0, local copies, waits for them, and re-layouts: 4.6 us -> none  [step(): lax.dynamic_index_in_dim(every, later_cycle, 0, keepdims=False)]
    ppermute x2 -> x0, starting transfers between devices: 2.69 us -> none  [the longest x1 2.63 us: with_halo(): lax.ppermute(lax.slice_in_dim(block, 0, width, axis=dim), axis, backward)]
    concatenate x1, local copies, waits for them, and re-layouts: 2.38 us -> 0.02 us  [on_device(): packed = jnp.concatenate(pieces, axis=1)]
    unnamed x7 -> x12, local copies, waits for them, and re-layouts: 1.76 us -> 3.94 us
  transfers between devices with their start and end apart: 3 -> 0, of which waited for: 2 -> 0; matrix products, arithmetic and copies ran while one was open for 2% -> 0% of each run, Pallas kernels for 0% -> 0%
where the time goes in v1:
time: 39.7 us; the launch traced here: 39.5 us
  Pallas kernels  32.6 us (82%)
  local copies, waits for them, and re-layouts  6.75 us (17%)
    pallas_call x1, Pallas kernels, on_device(): pl.pallas_call(functools.partial(smoother, members, channels, columns), o...  32.6 us
    unnamed x12, local copies, waits for them, and re-layouts  3.94 us
    slice x3, local copies, waits for them, and re-layouts, on_device(): piece = turned[:, begin:end].reshape(members, RIM_COLS * members)  1.38 us

profile of v1, /device:TPU:0, one launch (start us, length us, event | category | flops | bytes accessed | tf_op | source)
XLA Modules:
  0.0 39.5 jit_solution(3336231399494652154)
XLA Ops:
  0.0 0.0 copy-start
  0.0 1.1 %fusion.1 = (bf16[80,4,80]{0,1,2:T(4,128)(2,1)S(1)}, bf16[80,4,80]{0,1,2:T(4,128)(2,1)S(1)}) fusion(bf16[80,32,80]{0,1,2:T(8,128)(2,1)} %bitcast.11), kind=kLoop, calls=%fused_computation.6 | loop fusion | bytes 204800 | tf_op jit(solution)/shard_map/slice | solution.py:179
  1.1 0.1 copy.6
  1.3 0.1 reshape.19
  1.4 0.1 copy.5
  1.5 0.1 reshape.18
  1.7 0.0 copy-done
  1.7 0.2 fusion
  1.9 0.2 copy.9
  2.1 0.2 reshape.22
  2.2 0.2 copy.8
  2.4 0.2 reshape.21
  2.6 0.0 copy-start.1
  2.6 0.2 copy.7
  2.8 0.2 reshape.20
  3.0 0.7 %copy-done.1 = bf16[1,80,8,512]{3,2,1,0:T(8,128)(2,1)S(1)} copy-done((bf16[1,80,8,512]{3,2,1,0:T(8,128)(2,1)S(1)}, bf16[1,80,8,512]{3,2,1,0:T(8,128)(2,1)}, u32[]{:S(2)}) %copy-start.1) | copy-done | bytes 655384
  3.7 0.0 copy-start.2
  3.7 1.1 %copy.10 = bf16[10,8,8,512]{3,1,2,0:T(8,128)(2,1)} copy(bf16[10,8,8,512]{3,2,1,0:T(8,128)(2,1)S(1)} %bitcast.13) | data formatting | bytes 1310720
  4.7 0.0 copy-done.2
  4.7 32.6 %shard_map.46 = bf16[80,4096]{1,0:T(8,128)(2,1)} custom-call(bf16[80,2688]{1,0:T(8,128)(2,1)} %copy-done.2, bf16[80,4096]{1,0:T(8,128)(2,1)} %bitcast.10, s32[4,512]{1,0:T(4,128)} %idx_ref.1, f32[4,512]{1,0:T(4,128)} %wgt_ref.1), custom_call_target="tpu_custom_call" | custom-call | tf_op jit(solution)/shard_map/pallas_call | solution.py:187
  37.3 2.1 %copy.11 = bf16[10,8,8,512]{3,2,1,0:T(8,128)(2,1)} copy(bf16[10,8,8,512]{3,1,2,0:T(8,128)(2,1)} %bitcast.9) | data formatting | bytes 1310720
  (5 shorter events, 0.1 us)
Async XLA Ops:
  0.0 1.7 %copy-start = (bf16[1,80,80,32]{2,3,1,0:T(8,128)(2,1)S(1)}, bf16[1,80,80,32]{2,3,1,0:T(8,128)(2,1)}, u32[]{:S(2)}) copy-start(bf16[1,80,80,32]{2,3,1,0:T(8,128)(2,1)} %param.4) | copy-start | bytes 1228804
  2.6 1.1 %copy-start.1 = (bf16[1,80,8,512]{3,2,1,0:T(8,128)(2,1)S(1)}, bf16[1,80,8,512]{3,2,1,0:T(8,128)(2,1)}, u32[]{:S(2)}) copy-start(bf16[1,80,8,512]{3,2,1,0:T(8,128)(2,1)} %param.5) | copy-start | bytes 1966084
  3.7 1.1 %copy-start.2 = (bf16[80,2688]{1,0:T(8,128)(2,1)}, bf16[80,2688]{1,0:T(8,128)(2,1)S(1)}, u32[]{:S(2)}) copy-start(bf16[80,2688]{1,0:T(8,128)(2,1)S(1)} %constant_dynamic-update-slice_fusion.d_ref) | copy-start | bytes 1290244

commit v2 on v1

--- a/solution.py
+++ b/solution.py
@@ -9,6 +9,7 @@
 
 RIM_COLS = 4
 CHUNK = 8
+PIECES = 2
 MESH = pl.DeviceIdType.MESH
 
 
@@ -30,6 +31,22 @@
     return half, chunks, start
 
 
+def rows_of(members):
+    cuts = [min(members, round_up(members * i // PIECES, 16)) for i in range(PIECES + 1)]
+    return [(begin, end - begin) for begin, end in zip(cuts, cuts[1:]) if end > begin]
+
+
+def blocks_of(members, width, parts):
+    blocks = []
+    for start in range(0, width, 256):
+        end = min(width, start + 256)
+        offsets = [o for o, _ in parts if o < end and o + members > start]
+        low = min(offsets) // 128 * 128
+        high = min(width, round_up(max(offsets) + members, 128))
+        blocks.append((start, end - start, low, high - low))
+    return blocks
+
+
 def smoother(members, channels, columns, d_ref, ens_ref, idx_ref, wgt_ref, out_ref, *scratch):
     half, chunks, _ = plan_of(members, columns)
     held, sent, halo, table, total = scratch[:5]
@@ -46,13 +63,17 @@
         pl.semaphore_signal(barrier, inc=1, device_id=target, device_id_type=MESH)
     pl.semaphore_wait(barrier, 4)
 
-    def onward(number, source):
+    rows = rows_of(members)
+
+    def onward(number, piece, source):
         start, width, _ = chunks[number]
+        first, height = rows[piece]
+        where = (pl.ds(first, height), pl.ds(start, width))
         return pltpu.make_async_remote_copy(
-            src_ref=source.at[:, pl.ds(start, width)],
-            dst_ref=held.at[:, pl.ds(start, width)],
-            send_sem=send_sem.at[number],
-            recv_sem=recv_sem.at[number],
+            src_ref=source.at[where],
+            dst_ref=held.at[where],
+            send_sem=send_sem.at[number, piece],
+            recv_sem=recv_sem.at[number, piece],
             device_id={"cyc": before},
             device_id_type=MESH,
         )
@@ -73,7 +94,8 @@
     @pl.when(last)
     def _():
         for number in range(len(chunks)):
-            onward(number, d_ref).start()
+            for piece in range(len(rows)):
+                onward(number, piece, d_ref).start()
 
     @pl.when(inner)
     def _():
@@ -87,7 +109,7 @@
                     block.dtype
                 )
 
-    def apply(source, start, width, parts, first):
+    def apply(source, start, width, parts, first, begin, end):
         ends = [offset for offset, _ in parts[1:]] + [width]
 
         def channel(number, carry):
@@ -110,7 +132,7 @@
                 total[:, lanes] += product
             return carry
 
-        lax.fori_loop(0, channels, channel, 0)
+        lax.fori_loop(begin, end, channel, 0, unroll=4)
 
     @pl.when(jnp.logical_not(last))
     def _():
@@ -124,41 +146,71 @@
             )
         table[...] = entries
 
-    for number, (start, width, parts) in enumerate(chunks):
-
-        @pl.when(jnp.logical_not(last))
-        def _(number=number, start=start, width=width):
-            onward(number, d_ref).wait_recv()
-            if number == 0:
-                rim(0).start()
-                rim(1).start()
-
-        @pl.when(inner)
-        def _(number=number, start=start, width=width):
-            lanes = slice(start, start + width)
-            later = held[:, lanes]
-            product = jnp.dot(later, diag[number][...], preferred_element_type=jnp.float32)
-            product += later.astype(jnp.float32) + d_ref[:, lanes].astype(jnp.float32)
-            sent[:, lanes] = product.astype(sent.dtype)
-            onward(number, sent).start()
-
-        @pl.when(jnp.logical_not(last))
-        def _(number=number, start=start, width=width, parts=parts):
-            apply(
-                held, start, width, [(o, col + RIM_COLS) for o, col in parts], number == 0
-            )
-
-    @pl.when(jnp.logical_not(last))
-    def _():
+    def apply_chunk(number, begin=0, end=channels):
+        start, width, parts = chunks[number]
+        slots = [(offset, column + RIM_COLS) for offset, column in parts]
+        apply(held, start, width, slots, number == 0, begin, end)
+
+    def apply_rim():
         rim(0).wait_recv()
         rim(1).wait_recv()
         parts = [(i * members, i) for i in range(RIM_COLS)]
         parts += [(half + i * members, RIM_COLS + columns + i) for i in range(RIM_COLS)]
-        apply(halo, 0, 2 * half, parts, False)
+        apply(halo, 0, 2 * half, parts, False, 0, channels)
+
+    def finish():
         out_ref[...] = total[...].astype(out_ref.dtype)
         rim(0).wait_send()
         rim(1).wait_send()
 
+    def extend(number, piece):
+        start, width, parts = chunks[number]
+        first, height = rows[piece]
+        across = slice(first, first + height)
+        onward(number, piece, sent).wait_recv()
+        for lane, size, deep, depth in blocks_of(members, width, parts):
+            lanes = slice(start + lane, start + lane + size)
+            product = jnp.dot(
+                held[across, start + deep : start + deep + depth],
+                diag[number][deep : deep + depth, lane : lane + size],
+                preferred_element_type=jnp.float32,
+            )
+            product += held[across, lanes].astype(jnp.float32)
+            product += d_ref[across, lanes].astype(jnp.float32)
+            sent[across, lanes] = product.astype(sent.dtype)
+        onward(number, piece, sent).start()
+
+    @pl.when(inner)
+    def _():
+        for number in range(len(chunks)):
+            for piece in range(len(rows)):
+                extend(number, piece)
+                if number == 0 and piece == len(rows) - 1:
+                    rim(0).start()
+                    rim(1).start()
+                if number > 0:
+                    apply_chunk(
+                        number - 1,
+                        channels * piece // len(rows),
+                        channels * (piece + 1) // len(rows),
+                    )
+        apply_rim()
+        apply_chunk(len(chunks) - 1)
+        finish()
+
+    @pl.when(mine == 0)
+    def _():
+        for number in range(len(chunks)):
+            if number == len(chunks) - 1:
+                apply_rim()
+            for piece in range(len(rows)):
+                onward(number, piece, d_ref).wait_recv()
+            if number == 0:
+                rim(0).start()
+                rim(1).start()
+            apply_chunk(number)
+        finish()
+
     @pl.when(last)
     def _():
         out_ref[...] = ens_ref[...]
@@ -166,7 +218,8 @@
     @pl.when(mine > 0)
     def _():
         for number in range(len(chunks)):
-            onward(number, d_ref).wait_send()
+            for piece in range(len(rows)):
+                onward(number, piece, d_ref).wait_send()
 
 
 def on_device(weight_change, ensemble, stencil_index, stencil_weight):
@@ -198,8 +251,8 @@
         ]
         + [pltpu.VMEM((wide, wide), jnp.bfloat16) for _, wide, _ in chunks]
         + [
-            pltpu.SemaphoreType.DMA((len(chunks),)),
-            pltpu.SemaphoreType.DMA((len(chunks),)),
+            pltpu.SemaphoreType.DMA((len(chunks), PIECES)),
+            pltpu.SemaphoreType.DMA((len(chunks), PIECES)),
             pltpu.SemaphoreType.DMA((2,)),
             pltpu.SemaphoreType.DMA((2,)),
         ],

time: 39.7 us -> 35.3 us (0.89)
  Pallas kernels: 32.6 us -> 28.2 us
    pallas_call x1, Pallas kernels: 32.6 us -> 28.2 us  [on_device(): pl.pallas_call(functools.partial(smoother, members, channels, columns), o...]
where the time goes in v2:
time: 35.3 us; the launch traced here: 35 us
  Pallas kernels  28.2 us (80%)
  local copies, waits for them, and re-layouts  6.75 us (19%)
    pallas_call x1, Pallas kernels, on_device(): pl.pallas_call(functools.partial(smoother, members, channels, columns), o...  28.2 us
    unnamed x12, local copies, waits for them, and re-layouts  3.94 us
    slice x3, local copies, waits for them, and re-layouts, on_device(): piece = turned[:, begin:end].reshape(members, RIM_COLS * members)  1.38 us
    slice x4, local copies, waits for them, and re-layouts, on_device(): turned[:, parts[0][1]:parts[-1][1] + 1]  0.72 us

profile of v2, /device:TPU:0, one launch (start us, length us, event | category | flops | bytes accessed | tf_op | source)
XLA Modules:
  0.0 35.0 jit_solution(109644514123004715)
XLA Ops:
  0.0 0.0 copy-start
  0.0 1.1 %fusion.1 = (bf16[80,4,80]{0,1,2:T(4,128)(2,1)S(1)}, bf16[80,4,80]{0,1,2:T(4,128)(2,1)S(1)}) fusion(bf16[80,32,80]{0,1,2:T(8,128)(2,1)} %bitcast.11), kind=kLoop, calls=%fused_computation.6 | loop fusion | bytes 204800 | tf_op jit(solution)/shard_map/slice | solution.py:232
  1.1 0.1 copy.6
  1.3 0.1 reshape.19
  1.4 0.1 copy.5
  1.5 0.1 reshape.18
  1.7 0.0 copy-done
  1.7 0.2 fusion
  1.9 0.2 copy.9
  2.1 0.2 reshape.22
  2.2 0.2 copy.8
  2.4 0.2 reshape.21
  2.6 0.0 copy-start.1
  2.6 0.2 copy.7
  2.8 0.2 reshape.20
  3.0 0.7 %copy-done.1 = bf16[1,80,8,512]{3,2,1,0:T(8,128)(2,1)S(1)} copy-done((bf16[1,80,8,512]{3,2,1,0:T(8,128)(2,1)S(1)}, bf16[1,80,8,512]{3,2,1,0:T(8,128)(2,1)}, u32[]{:S(2)}) %copy-start.1) | copy-done | bytes 655384
  3.7 0.0 copy-start.2
  3.7 1.1 %copy.10 = bf16[10,8,8,512]{3,1,2,0:T(8,128)(2,1)} copy(bf16[10,8,8,512]{3,2,1,0:T(8,128)(2,1)S(1)} %bitcast.13) | data formatting | bytes 1310720
  4.7 0.0 copy-done.2
  4.7 28.2 %shard_map.46 = bf16[80,4096]{1,0:T(8,128)(2,1)} custom-call(bf16[80,2688]{1,0:T(8,128)(2,1)} %copy-done.2, bf16[80,4096]{1,0:T(8,128)(2,1)} %bitcast.10, s32[4,512]{1,0:T(4,128)} %idx_ref.1, f32[4,512]{1,0:T(4,128)} %wgt_ref.1), custom_call_target="tpu_custom_call" | custom-call | tf_op jit(solution)/shard_map/pallas_call | solution.py:240
  32.9 2.1 %copy.11 = bf16[10,8,8,512]{3,2,1,0:T(8,128)(2,1)} copy(bf16[10,8,8,512]{3,1,2,0:T(8,128)(2,1)} %bitcast.9) | data formatting | bytes 1310720
  (5 shorter events, 0.1 us)
Async XLA Ops:
  0.0 1.7 %copy-start = (bf16[1,80,80,32]{2,3,1,0:T(8,128)(2,1)S(1)}, bf16[1,80,80,32]{2,3,1,0:T(8,128)(2,1)}, u32[]{:S(2)}) copy-start(bf16[1,80,80,32]{2,3,1,0:T(8,128)(2,1)} %param.4) | copy-start | bytes 1228804
  2.6 1.1 %copy-start.1 = (bf16[1,80,8,512]{3,2,1,0:T(8,128)(2,1)S(1)}, bf16[1,80,8,512]{3,2,1,0:T(8,128)(2,1)}, u32[]{:S(2)}) copy-start(bf16[1,80,8,512]{3,2,1,0:T(8,128)(2,1)} %param.5) | copy-start | bytes 1966084
  3.7 1.1 %copy-start.2 = (bf16[80,2688]{1,0:T(8,128)(2,1)}, bf16[80,2688]{1,0:T(8,128)(2,1)S(1)}, u32[]{:S(2)}) copy-start(bf16[80,2688]{1,0:T(8,128)(2,1)S(1)} %constant_dynamic-update-slice_fusion.d_ref) | copy-start | bytes 1290244

commit v3 on v2

--- a/solution.py
+++ b/solution.py
@@ -47,11 +47,11 @@
     return blocks
 
 
-def smoother(members, channels, columns, d_ref, ens_ref, idx_ref, wgt_ref, out_ref, *scratch):
+def smoother(members, channels, columns, d_any, ens_any, idx_ref, wgt_ref, out_ref, *scratch):
     half, chunks, _ = plan_of(members, columns)
-    held, sent, halo, table, total = scratch[:5]
-    diag = scratch[5 : 5 + len(chunks)]
-    send_sem, recv_sem, halo_send, halo_recv = scratch[5 + len(chunks) :]
+    held, sent, halo, table, total, flat, d_ref, ens_ref = scratch[:8]
+    diag = scratch[8 : 8 + len(chunks)]
+    send_sem, recv_sem, halo_send, halo_recv, load_sem = scratch[8 + len(chunks) :]
     count, tiles = lax.axis_size("cyc"), lax.axis_size("tile")
     mine, tile = lax.axis_index("cyc"), lax.axis_index("tile")
     before, after = lax.rem(mine + count - 1, count), lax.rem(mine + 1, count)
@@ -61,6 +61,19 @@
     barrier = pltpu.get_barrier_semaphore()
     for target in ({"cyc": before}, {"cyc": after}, {"tile": left}, {"tile": right}):
         pl.semaphore_signal(barrier, inc=1, device_id=target, device_id_type=MESH)
+    last = mine == count - 1
+    inner = jnp.logical_and(mine > 0, mine < count - 1)
+    load_d = pltpu.make_async_copy(d_any, d_ref, load_sem.at[0])
+    load_states = pltpu.make_async_copy(ens_any, ens_ref, load_sem.at[1])
+
+    @pl.when(inner)
+    def _():
+        load_d.start()
+
+    @pl.when(jnp.logical_not(last))
+    def _():
+        load_states.start()
+
     pl.semaphore_wait(barrier, 4)
 
     rows = rows_of(members)
@@ -88,17 +101,15 @@
             device_id_type=MESH,
         )
 
-    last = mine == count - 1
-    inner = jnp.logical_and(mine > 0, mine < count - 1)
-
     @pl.when(last)
     def _():
         for number in range(len(chunks)):
             for piece in range(len(rows)):
-                onward(number, piece, d_ref).start()
+                onward(number, piece, d_any).start()
 
     @pl.when(inner)
     def _():
+        load_d.wait()
         for (start, width, parts), block in zip(chunks, diag):
             lane = lax.broadcasted_iota(jnp.int32, (members, width), 1)
             values = d_ref[:, start : start + width].astype(jnp.float32)
@@ -109,12 +120,12 @@
                     block.dtype
                 )
 
-    def apply(source, start, width, parts, first, begin, end):
+    def apply(source, start, width, parts, begin, end):
         ends = [offset for offset, _ in parts[1:]] + [width]
 
         def channel(number, carry):
             lanes = pl.ds(pl.multiple_of(number * points, points), points)
-            states = ens_ref[:, lanes]
+            states = flat[:, lanes]
             rows = []
             for (offset, slot), end in zip(parts, ends):
                 share = jnp.broadcast_to(table[slot : slot + 1, :], (members, points))
@@ -126,10 +137,10 @@
                 jnp.concatenate(rows, axis=0),
                 preferred_element_type=jnp.float32,
             )
-            if first:
-                total[:, lanes] = product + states.astype(jnp.float32)
-            else:
-                total[:, lanes] += product
+            for block in range(points // 128):
+                total[block, pl.ds(number, members, stride=channels), :] += product[
+                    :, block * 128 : (block + 1) * 128
+                ]
             return carry
 
         lax.fori_loop(begin, end, channel, 0, unroll=4)
@@ -145,21 +156,33 @@
                 idx_ref[corner : corner + 1, :] == slots, shares[corner : corner + 1, :], 0.0
             )
         table[...] = entries
+        load_states.wait()
+        for block in range(points // 128):
+            states = ens_ref[:, :, block * 128 : (block + 1) * 128].astype(jnp.float32)
+            total[block] = states.reshape(members * channels, 128)
+            for number in range(channels):
+                states = total[block, pl.ds(number, members, stride=channels), :]
+                begin = number * points + block * 128
+                flat[:, begin : begin + 128] = states.astype(flat.dtype)
+        total[...] = jnp.zeros_like(total)
 
     def apply_chunk(number, begin=0, end=channels):
         start, width, parts = chunks[number]
         slots = [(offset, column + RIM_COLS) for offset, column in parts]
-        apply(held, start, width, slots, number == 0, begin, end)
+        apply(held, start, width, slots, begin, end)
 
     def apply_rim():
         rim(0).wait_recv()
         rim(1).wait_recv()
         parts = [(i * members, i) for i in range(RIM_COLS)]
         parts += [(half + i * members, RIM_COLS + columns + i) for i in range(RIM_COLS)]
-        apply(halo, 0, 2 * half, parts, False, 0, channels)
+        apply(halo, 0, 2 * half, parts, 0, channels)
 
     def finish():
-        out_ref[...] = total[...].astype(out_ref.dtype)
+        for block in range(points // 128):
+            out_ref[:, :, block * 128 : (block + 1) * 128] = (
+                total[block].reshape(members, channels, 128).astype(out_ref.dtype)
+            )
         rim(0).wait_send()
         rim(1).wait_send()
 
@@ -204,7 +227,7 @@
             if number == len(chunks) - 1:
                 apply_rim()
             for piece in range(len(rows)):
-                onward(number, piece, d_ref).wait_recv()
+                onward(number, piece, sent).wait_recv()
             if number == 0:
                 rim(0).start()
                 rim(1).start()
@@ -213,13 +236,13 @@
 
     @pl.when(last)
     def _():
-        out_ref[...] = ens_ref[...]
+        out_ref[...] = jnp.zeros_like(out_ref)
 
     @pl.when(mine > 0)
     def _():
         for number in range(len(chunks)):
             for piece in range(len(rows)):
-                onward(number, piece, d_ref).wait_send()
+                onward(number, piece, sent).wait_send()
 
 
 def on_device(weight_change, ensemble, stencil_index, stencil_weight):
@@ -235,19 +258,23 @@
         piece = turned[:, parts[0][1] : parts[-1][1] + 1].reshape(members, len(parts) * members)
         pieces.append(jnp.pad(piece, ((0, 0), (0, wide - piece.shape[1]))))
     packed = jnp.concatenate(pieces, axis=1)
-    states = ensemble[0].reshape(members, channels * points)
+    states = ensemble[0]
     vmem = pl.BlockSpec(memory_space=pltpu.VMEM)
+    anywhere = pl.BlockSpec(memory_space=pl.ANY)
     result = pl.pallas_call(
         functools.partial(smoother, members, channels, columns),
-        out_shape=jax.ShapeDtypeStruct(states.shape, states.dtype),
-        in_specs=[vmem] * 4,
+        out_shape=pltpu.VMEM(states.shape, states.dtype),
+        in_specs=[vmem, anywhere] + [vmem] * 2,
         out_specs=vmem,
         scratch_shapes=[
             pltpu.VMEM((members, width), jnp.bfloat16),
             pltpu.VMEM((members, width), jnp.bfloat16),
             pltpu.VMEM((members, 2 * half), jnp.bfloat16),
             pltpu.VMEM((columns + 2 * RIM_COLS, points), jnp.float32),
-            pltpu.VMEM(states.shape, jnp.float32),
+            pltpu.VMEM((points // 128, members * channels, 128), jnp.float32),
+            pltpu.VMEM((members, channels * points), jnp.bfloat16),
+            pltpu.VMEM((members, width), jnp.bfloat16),
+            pltpu.VMEM(states.shape, jnp.bfloat16),
         ]
         + [pltpu.VMEM((wide, wide), jnp.bfloat16) for _, wide, _ in chunks]
         + [
@@ -255,10 +282,17 @@
             pltpu.SemaphoreType.DMA((len(chunks), PIECES)),
             pltpu.SemaphoreType.DMA((2,)),
             pltpu.SemaphoreType.DMA((2,)),
+            pltpu.SemaphoreType.DMA((2,)),
         ],
         compiler_params=pltpu.CompilerParams(collective_id=0, has_side_effects=True),
-    )(packed, states, stencil_index, stencil_weight)
-    return result.reshape(1, members, channels, points)
+    )(
+        pltpu.with_memory_space_constraint(packed, pltpu.VMEM),
+        states,
+        stencil_index,
+        stencil_weight,
+    )
+    total = states.astype(jnp.float32) + result.astype(jnp.float32)
+    return total.astype(states.dtype)[None]
 
 
 def solution(mesh):

time: 35.3 us -> 31.6 us (0.90)
  local copies, waits for them, and re-layouts: 6.75 us -> 2.89 us
  other arithmetic: 0 us -> 1.01 us
  Pallas kernels: 28.2 us -> 27.4 us
    unnamed x12 -> x8, local copies, waits for them, and re-layouts: 3.94 us -> 0.07 us
    broadcast_in_dim x0 -> x1, other arithmetic: none -> 1.01 us  [on_device(): return total.astype(states.dtype)[None]]
    pallas_call x1, Pallas kernels: 28.2 us -> 27.4 us  [on_device(): pl.pallas_call(functools.partial(smoother, members, channels, columns), o...]
where the time goes in v3:
time: 31.6 us; the launch traced here: 31.4 us
  Pallas kernels  27.4 us (87%)
  local copies, waits for them, and re-layouts  2.89 us (9%)
  other arithmetic  1.01 us (3%)
    pallas_call x1, Pallas kernels, on_device(): pl.pallas_call(functools.partial(smoother, members, channels, columns), o...  27.4 us
    slice x3, local copies, waits for them, and re-layouts, on_device(): piece = turned[:, begin:end].reshape(members, RIM_COLS * members)  1.38 us
    broadcast_in_dim x1, other arithmetic, on_device(): return total.astype(states.dtype)[None]  1.01 us
    slice x4, local copies, waits for them, and re-layouts, on_device(): turned[:, parts[0][1]:parts[-1][1] + 1]  0.72 us

profile of v3, /device:TPU:0, one launch (start us, length us, event | category | flops | bytes accessed | tf_op | source)
XLA Modules:
  0.0 31.4 jit_solution(16136519876072828364)
XLA Ops:
  0.0 0.0 copy-start.1
  0.0 1.1 %fusion.2 = (bf16[80,4,80]{0,1,2:T(4,128)(2,1)S(1)}, bf16[80,4,80]{0,1,2:T(4,128)(2,1)S(1)}) fusion(bf16[80,32,80]{0,1,2:T(8,128)(2,1)} %bitcast.8), kind=kLoop, calls=%fused_computation.8 | loop fusion | bytes 204800 | tf_op jit(solution)/shard_map/slice | solution.py:255
  1.1 0.1 copy.6
  1.3 0.1 reshape.16
  1.4 0.1 copy.5
  1.5 0.1 reshape.15
  1.7 0.0 copy-done.1
  1.7 0.2 fusion.1
  1.9 0.2 copy.9
  2.1 0.2 reshape.19
  2.2 0.2 copy.8
  2.4 0.2 reshape.18
  2.6 0.2 copy.7
  2.8 0.2 reshape.17
  3.0 0.0 copy-start
  3.0 27.4 %shard_map.46 = bf16[80,8,512]{2,1,0:T(8,128)(2,1)S(1)} custom-call(bf16[80,2688]{1,0:T(8,128)(2,1)S(1)} %constant_dynamic-update-slice_fusion.d_any, bf16[80,8,512]{2,1,0:T(8,128)(2,1)} %bitcast.7, s32[4,512]{1,0:T(4,128)} %idx_ref.1, f32[4,512]{1,0:T(4,128)} %wgt_ref.1), custom_call_target="tpu_custom_call" | custom-call | tf_op jit(solution)/shard_map/pallas_call | solution.py:264
  30.4 0.0 copy-done
  30.4 1.0 %fusion = bf16[1,80,8,512]{3,2,1,0:T(8,128)(2,1)} fusion(bf16[80,8,512]{2,1,0:T(8,128)(2,1)S(1)} %shard_map.46, bf16[1,80,8,512]{3,2,1,0:T(8,128)(2,1)S(1)} %copy-done), kind=kLoop, calls=%fused_computation.1 | loop fusion | flops 1310720 | bytes 1966080 | tf_op jit(solution)/shard_map/broadcast_in_dim | solution.py:295
  (5 shorter events, 0.1 us)
Async XLA Ops:
  0.0 1.7 %copy-start.1 = (bf16[1,80,80,32]{2,3,1,0:T(8,128)(2,1)S(1)}, bf16[1,80,80,32]{2,3,1,0:T(8,128)(2,1)}, u32[]{:S(2)}) copy-start(bf16[1,80,80,32]{2,3,1,0:T(8,128)(2,1)} %param.4) | copy-start | bytes 1228804
  3.0 27.4 %copy-start = (bf16[1,80,8,512]{3,2,1,0:T(8,128)(2,1)S(1)}, bf16[1,80,8,512]{3,2,1,0:T(8,128)(2,1)}, u32[]{:S(2)}) copy-start(bf16[1,80,8,512]{3,2,1,0:T(8,128)(2,1)} %param.5) | copy-start | bytes 1966084

commit v4 on v3

--- a/solution.py
+++ b/solution.py
@@ -9,7 +9,7 @@
 
 RIM_COLS = 4
 CHUNK = 8
-PIECES = 2
+PIECES = 3
 MESH = pl.DeviceIdType.MESH
 
 
@@ -205,20 +205,23 @@
 
     @pl.when(inner)
     def _():
+        middle = channels // 2
+        tasks = [
+            (number, begin, end)
+            for number in range(len(chunks))
+            for begin, end in ((0, middle), (middle, channels))
+        ]
         for number in range(len(chunks)):
             for piece in range(len(rows)):
                 extend(number, piece)
                 if number == 0 and piece == len(rows) - 1:
                     rim(0).start()
                     rim(1).start()
-                if number > 0:
-                    apply_chunk(
-                        number - 1,
-                        channels * piece // len(rows),
-                        channels * (piece + 1) // len(rows),
-                    )
+                if piece in (1,) and tasks and tasks[0][0] < number - 0:
+                    apply_chunk(*tasks.pop(0))
         apply_rim()
-        apply_chunk(len(chunks) - 1)
+        for task in tasks:
+            apply_chunk(*task)
         finish()
 
     @pl.when(mine == 0)

time: 31.6 us -> 31.3 us (level)
  no operation moved by 1% of the time
where the time goes in v4:
time: 31.3 us; the launch traced here: 31.1 us
  Pallas kernels  27.1 us (87%)
  local copies, waits for them, and re-layouts  2.89 us (9%)
  other arithmetic  1.01 us (3%)
    pallas_call x1, Pallas kernels, on_device(): pl.pallas_call(functools.partial(smoother, members, channels, columns), o...  27.1 us
    slice x3, local copies, waits for them, and re-layouts, on_device(): piece = turned[:, begin:end].reshape(members, RIM_COLS * members)  1.38 us
    broadcast_in_dim x1, other arithmetic, on_device(): return total.astype(states.dtype)[None]  1.01 us
    slice x4, local copies, waits for them, and re-layouts, on_device(): turned[:, parts[0][1]:parts[-1][1] + 1]  0.72 us

profile of v4, /device:TPU:0, one launch (start us, length us, event | category | flops | bytes accessed | tf_op | source)
XLA Modules:
  0.0 31.1 jit_solution(6503895441620295674)
XLA Ops:
  0.0 0.0 copy-start.1
  0.0 1.1 %fusion.2 = (bf16[80,4,80]{0,1,2:T(4,128)(2,1)S(1)}, bf16[80,4,80]{0,1,2:T(4,128)(2,1)S(1)}) fusion(bf16[80,32,80]{0,1,2:T(8,128)(2,1)} %bitcast.8), kind=kLoop, calls=%fused_computation.8 | loop fusion | bytes 204800 | tf_op jit(solution)/shard_map/slice | solution.py:258
  1.1 0.1 copy.6
  1.3 0.1 reshape.16
  1.4 0.1 copy.5
  1.5 0.1 reshape.15
  1.7 0.0 copy-done.1
  1.7 0.2 fusion.1
  1.9 0.2 copy.9
  2.1 0.2 reshape.19
  2.2 0.2 copy.8
  2.4 0.2 reshape.18
  2.6 0.2 copy.7
  2.8 0.2 reshape.17
  3.0 0.0 copy-start
  3.0 27.1 %shard_map.46 = bf16[80,8,512]{2,1,0:T(8,128)(2,1)S(1)} custom-call(bf16[80,2688]{1,0:T(8,128)(2,1)S(1)} %constant_dynamic-update-slice_fusion.d_any, bf16[80,8,512]{2,1,0:T(8,128)(2,1)} %bitcast.7, s32[4,512]{1,0:T(4,128)} %idx_ref.1, f32[4,512]{1,0:T(4,128)} %wgt_ref.1), custom_call_target="tpu_custom_call" | custom-call | tf_op jit(solution)/shard_map/pallas_call | solution.py:267
  30.1 0.0 copy-done
  30.1 1.0 %fusion = bf16[1,80,8,512]{3,2,1,0:T(8,128)(2,1)} fusion(bf16[80,8,512]{2,1,0:T(8,128)(2,1)S(1)} %shard_map.46, bf16[1,80,8,512]{3,2,1,0:T(8,128)(2,1)S(1)} %copy-done), kind=kLoop, calls=%fused_computation.1 | loop fusion | flops 1310720 | bytes 1966080 | tf_op jit(solution)/shard_map/broadcast_in_dim | solution.py:298
  (5 shorter events, 0.1 us)
Async XLA Ops:
  0.0 1.7 %copy-start.1 = (bf16[1,80,80,32]{2,3,1,0:T(8,128)(2,1)S(1)}, bf16[1,80,80,32]{2,3,1,0:T(8,128)(2,1)}, u32[]{:S(2)}) copy-start(bf16[1,80,80,32]{2,3,1,0:T(8,128)(2,1)} %param.4) | copy-start | bytes 1228804
  3.0 27.1 %copy-start = (bf16[1,80,8,512]{3,2,1,0:T(8,128)(2,1)S(1)}, bf16[1,80,8,512]{3,2,1,0:T(8,128)(2,1)}, u32[]{:S(2)}) copy-start(bf16[1,80,8,512]{3,2,1,0:T(8,128)(2,1)} %param.5) | copy-start | bytes 1966084
